TPU v7x, 32 devices: a whole 2x2x4 slice. The times are simulated.
32 devices in a mesh: gx: 4 (over z), gy: 4 (over y, core), gz: 2 (over x).
Axes of the slice: x: 2, y: 2, z: 4, core: 2. Of those that a mesh axis runs over, the one named last changes fastest.
Arguments:
- node_irreps: bfloat16 [4, 4, 2, 16, 25, 128], P('gx', 'gy', 'gz'), may hold values from -5 to 11
- positions: float32 [4, 4, 2, 3, 16], P('gx', 'gy', 'gz'), may hold values from 0 to 6.8
- send_list: int32 [4, 4, 2, 8], P('gx', 'gy', 'gz'), may hold values from 0 to 15, as said below
- neighbours: int32 [4, 4, 2, 16, 32], P('gx', 'gy', 'gz'), may hold values from 0 to 231
- displacements: float32 [4, 4, 2, 3, 512], P('gx', 'gy', 'gz'), may hold values from -6 to 6
- order_zero: bfloat16 [640, 640], replicated, may hold values from -0.25 to 0.25
- order_one: bfloat16 [512, 1024], replicated, may hold values from -0.25 to 0.25
- order_two: bfloat16 [384, 768], replicated, may hold values from -0.3125 to 0.3125
- reciprocal_triples: int32 [1024, 3], replicated, may hold values from -6 to 6
- reciprocal_filter: float32 [1024, 128], replicated, may hold values from 0.1 to 1
- cotangent: float32 [4, 4, 2, 16, 128], P('gx', 'gy', 'gz'), may hold values from -5 to 11
Outputs:
- updated: bfloat16 [4, 4, 2, 16, 25, 128], P('gx', 'gy', 'gz')
- long_range: float32 [4, 4, 2, 16, 128], P('gx', 'gy', 'gz')
- charge_grad: float32 [4, 4, 2, 16, 128], P('gx', 'gy', 'gz')
- position_grad: float32 [4, 4, 2, 3, 16], P('gx', 'gy', 'gz')
Inputs may be any that keep to these rules, and one draw needn't show every extreme that they name: `send_list`: entries of one block are distinct atoms of that block.
All inputs are finite; a program needn't handle non-finite values.
Results may differ from a plain program's by a relative error of at most 0.0023.
Values may be sent and summed in bfloat16 or wider, within the bound.
No kernel may reach another device: no remote copies, remote signals or barrier semaphores. Data moves between devices by JAX's collectives and lax.ppermute only.
A program may use at most 64 MiB of HBM per device.

v0:
```python
import math
import jax
import jax.numpy as jnp
from jax import lax
from jax.sharding import PartitionSpec as P

highest = lax.Precision.HIGHEST
cell_length = 6.8
planar_floor = 0.25
radial_width = 64.0


def with_halo(block, sides, width):
    for axis, dim in sides:
        count = lax.axis_size(axis)
        forward = [(i, i + 1) for i in range(count - 1)]
        forward.append((count - 1, 0))
        backward = [(target, source) for source, target in forward]
        low = lax.ppermute(
            lax.slice_in_dim(block, block.shape[dim] - width, None, axis=dim), axis, forward
        )
        high = lax.ppermute(lax.slice_in_dim(block, 0, width, axis=dim), axis, backward)
        block = jnp.concatenate([low, block, high], axis=dim)
    return block


def harmonic_slot(degree, signed_order):
    return degree * degree + degree + signed_order


def kept_rows():
    layout = []
    for degree in range(5):
        for signed_order in range(-degree, degree + 1):
            layout.append(harmonic_slot(degree, signed_order))
    return layout


def edge_messages(
    lookup_table, displacement, neighbour_index, order_zero, order_one, order_two, layout
):
    atom_count = neighbour_index.shape[0]
    neighbour_count = neighbour_index.shape[1]
    flat_index = neighbour_index.reshape(-1)
    edge_count = flat_index.shape[0]
    feature_width = lookup_table.shape[2]
    source = lookup_table[flat_index]
    length_squared = jnp.sum(displacement * displacement, axis=0)
    radial = jnp.exp(-length_squared / radial_width) / math.sqrt(neighbour_count)
    planar = jnp.sqrt(
        displacement[0] * displacement[0] + displacement[1] * displacement[1] + planar_floor
    )
    cos_one = displacement[0] / planar
    sin_one = displacement[1] / planar

    def neighbour_sum(values):
        weighted = values * radial[:, None, None]
        return jnp.sum(
            weighted.reshape(atom_count, neighbour_count, values.shape[1], feature_width), axis=1
        )

    collected = {}
    zero_slots = [layout.index(harmonic_slot(degree, 0)) for degree in range(5)]
    zero_input = source[:, zero_slots, :].reshape(edge_count, 5 * feature_width)
    zero_output = jnp.dot(zero_input, order_zero, preferred_element_type=jnp.float32)
    summed_zero_part = neighbour_sum(zero_output.reshape(edge_count, 5, feature_width))
    for degree in range(5):
        collected[harmonic_slot(degree, 0)] = summed_zero_part[:, degree]
    rotations = (
        (1, cos_one, sin_one, order_one),
        (2, cos_one * cos_one - sin_one * sin_one, 2.0 * cos_one * sin_one, order_two),
    )
    for harmonic_order, cosine, sine_term, weight_pair in rotations:
        degrees = list(range(harmonic_order, 5))
        count_of_rows = len(degrees)
        plus_slots = [layout.index(harmonic_slot(degree, harmonic_order)) for degree in degrees]
        minus_slots = [layout.index(harmonic_slot(degree, -harmonic_order)) for degree in degrees]
        plus_part = source[:, plus_slots, :].astype(jnp.float32)
        minus_part = source[:, minus_slots, :].astype(jnp.float32)
        cosine_wide = cosine[:, None, None]
        sine_wide = sine_term[:, None, None]
        turned_plus = (cosine_wide * plus_part + sine_wide * minus_part).astype(jnp.bfloat16)
        turned_minus = (cosine_wide * minus_part - sine_wide * plus_part).astype(jnp.bfloat16)
        split_at = count_of_rows * feature_width
        stacked = jnp.concatenate(
            [turned_plus.reshape(edge_count, split_at), turned_minus.reshape(edge_count, split_at)],
            axis=0,
        )
        product = jnp.dot(stacked, weight_pair, preferred_element_type=jnp.float32)
        upper_half = product[:edge_count]
        lower_half = product[edge_count:]
        mixed_plus = (upper_half[:, :split_at] - lower_half[:, split_at:]).reshape(
            edge_count, count_of_rows, feature_width
        )
        mixed_minus = (upper_half[:, split_at:] + lower_half[:, :split_at]).reshape(
            edge_count, count_of_rows, feature_width
        )
        back_plus = neighbour_sum(cosine_wide * mixed_plus - sine_wide * mixed_minus)
        back_minus = neighbour_sum(sine_wide * mixed_plus + cosine_wide * mixed_minus)
        for position_in, degree in enumerate(degrees):
            collected[harmonic_slot(degree, harmonic_order)] = back_plus[:, position_in]
            collected[harmonic_slot(degree, -harmonic_order)] = back_minus[:, position_in]
    zero_block = jnp.zeros((atom_count, feature_width), jnp.float32)
    return jnp.stack([collected.get(slot_number, zero_block) for slot_number in range(25)], axis=1)


def table_product(table, values):
    return jnp.dot(table.T, values, precision=highest)


def local(
    node_irreps,
    positions,
    send_list,
    neighbours,
    displacements,
    order_zero,
    order_one,
    order_two,
    reciprocal_triples,
    reciprocal_filter,
    cotangent,
):
    local_irreps = node_irreps[0, 0, 0]
    atom_count = local_irreps.shape[0]
    size_x = lax.axis_size("gx")
    size_y = lax.axis_size("gy")
    size_z = lax.axis_size("gz")
    total_atom_count = atom_count * size_x * size_y * size_z
    scale_factor = 1.0 / math.sqrt(total_atom_count * reciprocal_filter.shape[0])
    corner = jnp.stack([lax.axis_index("gx"), lax.axis_index("gy"), lax.axis_index("gz")]).astype(
        jnp.float32
    )
    box = cell_length * jnp.array([size_x, size_y, size_z], jnp.float32)
    fractional = (positions[0, 0, 0] + cell_length * corner[:, None]) / box[:, None]
    wave_float = reciprocal_triples.astype(jnp.float32)
    phase = 2.0 * math.pi * jnp.dot(fractional.T, wave_float.T, precision=highest)
    cos_table = jnp.cos(phase)
    sin_table = jnp.sin(phase)
    charges = local_irreps[:, 0, :].astype(jnp.float32)
    grad_input = cotangent[0, 0, 0]
    raw_cos, raw_sin, charge_total, plane_cos, plane_sin = lax.psum(
        (
            table_product(cos_table, charges),
            table_product(sin_table, charges),
            jnp.sum(charges, axis=0),
            jnp.sum(cos_table, axis=0),
            jnp.sum(sin_table, axis=0),
        ),
        ("gx", "gy", "gz"),
    )
    resp_cos, resp_sin = lax.psum(
        (table_product(cos_table, grad_input), table_product(sin_table, grad_input)),
        ("gx", "gy", "gz"),
    )
    mean_charge = charge_total / total_atom_count
    centered = charges - mean_charge
    struct_cos = raw_cos - plane_cos[:, None] * mean_charge[None, :]
    struct_sin = raw_sin - plane_sin[:, None] * mean_charge[None, :]
    sent_rows = send_list[0, 0, 0]
    layout = kept_rows()
    arrived = with_halo(
        local_irreps[sent_rows][None, None, None], (("gx", 0), ("gy", 1), ("gz", 2)), 1
    )
    ghost_table = arrived.reshape((-1,) + local_irreps.shape[1:])
    lookup_table = jnp.concatenate([local_irreps, ghost_table], axis=0)
    messages = edge_messages(
        lookup_table,
        displacements[0, 0, 0],
        neighbours[0, 0, 0],
        order_zero,
        order_one,
        order_two,
        layout,
    )
    updated = (local_irreps.astype(jnp.float32) + messages).astype(jnp.bfloat16)
    long_range = scale_factor * (
        jnp.dot(cos_table, reciprocal_filter * struct_cos, precision=highest)
        + jnp.dot(sin_table, reciprocal_filter * struct_sin, precision=highest)
    )
    charge_term = scale_factor * (
        jnp.dot(cos_table, reciprocal_filter * resp_cos, precision=highest)
        + jnp.dot(sin_table, reciprocal_filter * resp_sin, precision=highest)
    )
    term_mean = (
        scale_factor
        * (
            jnp.dot(plane_cos, reciprocal_filter * resp_cos, precision=highest)
            + jnp.dot(plane_sin, reciprocal_filter * resp_sin, precision=highest)
        )
        / total_atom_count
    )
    charge_grad = charge_term - term_mean
    with_sin = jnp.dot(grad_input, (reciprocal_filter * struct_sin).T, precision=highest) + jnp.dot(
        centered, (reciprocal_filter * resp_sin).T, precision=highest
    )
    with_cos = jnp.dot(grad_input, (reciprocal_filter * struct_cos).T, precision=highest) + jnp.dot(
        centered, (reciprocal_filter * resp_cos).T, precision=highest
    )
    phase_grad = scale_factor * (cos_table * with_sin - sin_table * with_cos)
    position_grad = (2.0 * math.pi * jnp.dot(phase_grad, wave_float, precision=highest) / box).T
    return (
        updated[None, None, None],
        long_range[None, None, None],
        charge_grad[None, None, None],
        position_grad[None, None, None],
    )


def solution(mesh):
    return jax.shard_map(
        local,
        mesh=mesh,
        in_specs=(
            P("gx", "gy", "gz", None, None, None),
            P("gx", "gy", "gz", None, None),
            P("gx", "gy", "gz", None),
            P("gx", "gy", "gz", None, None),
            P("gx", "gy", "gz", None, None),
            P(),
            P(),
            P(),
            P(),
            P(),
            P("gx", "gy", "gz", None, None),
        ),
        out_specs=(
            P("gx", "gy", "gz", None, None, None),
            P("gx", "gy", "gz", None, None),
            P("gx", "gy", "gz", None, None),
            P("gx", "gy", "gz", None, None),
        ),
        check_vma=False,
    )
```

profile of v0, /device:TPU:0, one launch (start us, length us, event | category | flops | bytes accessed | tf_op | source)
XLA Modules:
  0.0 176.4 jit_solution(5121559690905927124)
XLA Ops:
  9.5 5.1 %collective-permute-start.1 = (bf16[1,1,1,8,25,128]{5,4,3,2,1,0:T(8,128)(2,1)S(1)}, bf16[1,1,1,8,25,128]{5,4,3,2,1,0:T(8,128)(2,1)S(1)}, u32[]{:S(2)}, u32[]{:S(2)}) collective-permute-start(bf16[1,1,1,8,25,128]{5,4,3,2,1,0:T(8,128)(2,1)S(1)} %bitcast.173), channel_id=1, source_target_pairs={{8,0},{16,8},{24,16},{0,24},{9,1},{17,9},{25,17},{1,25},{10,2},{18... | collective-permute-start | bytes 153608 | tf_op jit(solution)/shard_map/ppermute | solution.py:22
  18.9 2.5 %fusion.34 = f32[1024,128]{1,0:T(8,128)} fusion(f32[16,1024]{1,0:T(8,128)S(1)} %get-tuple-element.43, f32[1,1,1,16,128]{4,3,2,1,0:T(8,128)} %param.27), kind=kOutput, calls=%fused_computation.112 | convolution fusion | flops 25165824 | bytes 598016 | tf_op jit(solution)/shard_map/dot_general | solution.py:108
  21.4 1.8 %fusion.36 = f32[1024,128]{1,0:T(8,128)} fusion(f32[16,1024]{1,0:T(8,128)S(1)} %get-tuple-element.44, f32[1,1,1,16,128]{4,3,2,1,0:T(8,128)S(1)} %copy-done.11), kind=kOutput, calls=%fused_computation.114 | convolution fusion | flops 25165824 | bytes 598016 | tf_op jit(solution)/shard_map/dot_general | solution.py:108
  23.5 40.4 %all-reduce = (f32[128]{0:T(128)S(1)}, f32[1024]{0:T(1024)S(1)}, f32[1024]{0:T(1024)S(1)}) all-reduce(f32[128]{0:T(128)S(1)} %get-tuple-element.33, f32[1024]{0:T(1024)S(1)} %reduce_sum.87, f32[1024]{0:T(1024)S(1)} %reduce_sum.89), channel_id=1, replica_groups=mesh['gx'=4,'gy'=4,'gz'=2] {'gx','gy','gz'}, use_global_device_ids=true, to_apply=%region_10.0 | all-reduce | flops 2176 | bytes 17408 | tf_op jit(solution)/shard_map/psum | solution.py:142
  64.5 3.0 %collective-permute-done.3 = bf16[3,1,1,8,25,128]{5,4,3,2,1,0:T(8,128)(2,1)S(1)} collective-permute-done((bf16[3,1,1,8,25,128]{5,4,3,2,1,0:T(8,128)(2,1)S(1)}, bf16[3,1,1,8,25,128]{5,4,3,2,1,0:T(8,128)(2,1)S(1)}, u32[]{:S(2)}, u32[]{:S(2)}) %collective-permute-start.3) | collective-permute-done | bytes 153632 | tf_op jit(solution)/shard_map/ppermute | solution.py:22
  67.5 4.2 %collective-permute-done.2 = bf16[3,1,1,8,25,128]{5,4,3,2,1,0:T(8,128)(2,1)S(1)} collective-permute-done((bf16[3,1,1,8,25,128]{5,4,3,2,1,0:T(8,128)(2,1)S(1)}, bf16[3,1,1,8,25,128]{5,4,3,2,1,0:T(8,128)(2,1)S(1)}, u32[]{:S(2)}, u32[]{:S(2)}) %collective-permute-start.2) | collective-permute-done | bytes 153632 | tf_op jit(solution)/shard_map/ppermute | solution.py:19
  77.1 8.9 %collective-permute-done.5 = bf16[3,3,1,8,25,128]{5,3,4,2,1,0:T(8,128)(2,1)} collective-permute-done((bf16[3,3,1,8,25,128]{5,3,4,2,1,0:T(8,128)(2,1)S(1)}, bf16[3,3,1,8,25,128]{5,3,4,2,1,0:T(8,128)(2,1)}, u32[]{:S(2)}, u32[]{:S(2)}) %collective-permute-start.5) | collective-permute-done | bytes 460832 | tf_op jit(solution)/shard_map/ppermute | solution.py:22
  87.1 8.1 %collective-permute-done.4 = bf16[3,3,1,8,25,128]{5,3,4,2,1,0:T(8,128)(2,1)} collective-permute-done((bf16[3,3,1,8,25,128]{5,3,4,2,1,0:T(8,128)(2,1)S(1)}, bf16[3,3,1,8,25,128]{5,3,4,2,1,0:T(8,128)(2,1)}, u32[]{:S(2)}, u32[]{:S(2)}) %collective-permute-start.4) | collective-permute-done | bytes 460832 | tf_op jit(solution)/shard_map/ppermute | solution.py:19
  96.9 3.5 %gather_fusion.1 = bf16[512,25,128]{2,1,0:T(8,128)(2,1)} fusion(bf16[232,25,128]{2,1,0:T(8,128)(2,1)S(1)} %pad_maximum_fusion, s32[1024]{0:T(1024)S(1)} %get-tuple-element.75), kind=kCustom, calls=%fused_computation.1 | custom fusion | bytes 6555648 | tf_op jit(solution)/shard_map/gather | solution.py:47
  100.3 5.2 %copy.56 = bf16[512,25,128]{2,0,1:T(8,128)(2,1)} copy(bf16[512,25,128]{2,1,0:T(8,128)(2,1)} %gather_fusion.1) | data formatting | bytes 6553600 | tf_op jit(solution)/shard_map/gather | solution.py:47
  105.5 3.3 %gather_fusion.6 = bf16[3,512,128]{2,1,0:T(8,128)(2,1)} fusion(bf16[512,25,128]{2,0,1:T(8,128)(2,1)} %copy.56, s32[1024]{0:T(1024)S(1)} %get-tuple-element.70), kind=kCustom, calls=%fused_computation.6 | custom fusion | bytes 786444 | tf_op jit(solution)/shard_map/gather | solution.py:79
  108.8 2.5 %gather_fusion.5 = bf16[3,512,128]{2,1,0:T(8,128)(2,1)S(1)} fusion(bf16[512,25,128]{2,0,1:T(8,128)(2,1)} %copy.56, s32[1024]{0:T(1024)S(1)} %get-tuple-element.71), kind=kCustom, calls=%fused_computation.5 | custom fusion | bytes 786444 | tf_op jit(solution)/shard_map/gather | solution.py:78
  113.9 3.4 %gather_fusion.4 = bf16[4,512,128]{2,1,0:T(8,128)(2,1)} fusion(bf16[512,25,128]{2,0,1:T(8,128)(2,1)} %copy.56, s32[1024]{0:T(1024)S(1)} %get-tuple-element.72), kind=kCustom, calls=%fused_computation.4 | custom fusion | bytes 1048592 | tf_op jit(solution)/shard_map/gather | solution.py:79
  117.3 3.4 %gather_fusion.3 = bf16[4,512,128]{2,1,0:T(8,128)(2,1)} fusion(bf16[512,25,128]{2,0,1:T(8,128)(2,1)} %copy.56, s32[1024]{0:T(1024)S(1)} %get-tuple-element.73), kind=kCustom, calls=%fused_computation.3 | custom fusion | bytes 1048592 | tf_op jit(solution)/shard_map/gather | solution.py:78
  120.7 2.6 %gather_fusion.2 = bf16[5,512,128]{2,1,0:T(8,128)(2,1)S(1)} fusion(bf16[512,25,128]{2,0,1:T(8,128)(2,1)} %copy.56, s32[1024]{0:T(1024)S(1)} %get-tuple-element.74), kind=kCustom, calls=%fused_computation.2 | custom fusion | bytes 1310740 | tf_op jit(solution)/shard_map/gather | solution.py:64
  124.4 2.2 %bitcast_reduce_fusion = f32[16,5,128]{2,0,1:T(8,128)S(1)} fusion(f32[512]{0:T(512)S(1)} %exponential_multiply_fusion, bf16[512,640,1]{0,1,2:T(8,128)(2,1)} %bitcast.182, bf16[5,128,640]{2,1,0:T(8,128)(2,1)} %bitcast.181), kind=kOutput, calls=%fused_computation.10 | convolution fusion | flops 420075520 | bytes 1517568 | tf_op jit(solution)/shard_map/dot_general | solution.py:65
  135.8 3.1 %multiply_reduce_fusion = (f32[16,3,128]{2,1,0:T(4,128)S(1)}, f32[16,3,128]{2,1,0:T(4,128)S(1)}) fusion(f32[16,32,3,128]{3,2,1,0:T(4,128)S(1)} %reshape.294, f32[16,32,3,128]{3,2,1,0:T(4,128)S(1)} %reshape.293, f32[16,32]{1,0:T(8,128)S(1)} %div.88, f32[16,32]{1,0:T(8,128)} %get-tuple-element.60, f32[16,32]{1,0:T(8,128)} %get-tuple-element.59), kind=kLoop, calls=%fused_computation.50 | loop fusion | flops 1953792 | bytes 1628160 | tf_op jit(solution)/shard_map/reduce_sum | solution.py:58
  140.6 1.8 %slice_subtract_fusion = (f32[512,512]{1,0:T(8,128)}, f32[512,512]{1,0:T(8,128)}) fusion(f32[1024,1024]{1,0:T(8,128)S(1)} %fusion.13), kind=kLoop, calls=%fused_computation.35 | loop fusion | flops 524288 | bytes 6291456 | tf_op jit(solution)/shard_map/sub | solution.py:92
  142.4 1.6 reshape.291
  144.1 2.6 %reshape.292 = f32[16,32,4,128]{3,2,1,0:T(4,128)} reshape(f32[512,512]{1,0:T(8,128)} %get-tuple-element.36) | data formatting | bytes 2097152 | tf_op jit(solution)/shard_map/reshape | solution.py:95
  146.7 3.7 %multiply_reduce_fusion.2 = (f32[16,4,128]{2,1,0:T(4,128)S(1)}, f32[16,4,128]{2,1,0:T(4,128)S(1)}) fusion(f32[16,32,4,128]{3,2,1,0:T(4,128)} %reshape.292, f32[16,32,4,128]{3,2,1,0:T(4,128)S(1)} %reshape.291, f32[16,32]{1,0:T(8,128)S(1)} %div.88, f32[16,32]{1,0:T(8,128)S(1)} %copy-done.13, f32[16,32]{1,0:T(8,128)S(1)} %copy-done.14), kind=kLoop, calls=%fused_computation.52 | loop fusion | flops 2605056 | bytes 2168832 | tf_op jit(solution)/shard_map/reduce_sum | solution.py:58
  151.3 8.9 %all-reduce.4.cloned.1.call-done = (f32[1024,128]{1,0:T(8,128)}, f32[1024,128]{1,0:T(8,128)}, f32[1024,128]{1,0:T(8,128)}, f32[1024,128]{1,0:T(8,128)}) async-done(((f32[1024,128]{1,0:T(8,128)}, f32[1024,128]{1,0:T(8,128)}, f32[1024,128]{1,0:T(8,128)}, f32[1024,128]{1,0:T(8,128)}), (f32[1024,128]{1,0:T(8,128)}, f32[1024,128]{1,0:T(8,128)}, f32[1024,128]{1,0:T(8,128)}, ...) | async-done | bytes 2097168 | tf_op jit(solution)/shard_map/psum | solution.py:142
  160.3 1.6 fusion.29
  161.8 1.7 convolution_bitcast_fusion
  (151 shorter events, 36.6 us)
Async XLA Ops:
  7.2 132.1 %copy-start = (bf16[512,1024]{1,0:T(8,128)(2,1)S(1)}, bf16[512,1024]{1,0:T(8,128)(2,1)}, u32[]{:S(2)}) copy-start(bf16[512,1024]{1,0:T(8,128)(2,1)} %param.23) | copy-start | bytes 3145732
  7.2 14.2 %copy-start.11 = (f32[1,1,1,16,128]{4,3,2,1,0:T(8,128)S(1)}, f32[1,1,1,16,128]{4,3,2,1,0:T(8,128)}, u32[]{:S(2)}) copy-start(f32[1,1,1,16,128]{4,3,2,1,0:T(8,128)} %param.27) | copy-start | bytes 24580
  7.2 153.1 %all-reduce.4.cloned.1.call-start = ((), (), s32[]{:S(2)}) async-start(), calls=%async_computation | async-start | bytes 4194304 | tf_op jit(solution)/shard_map/psum | solution.py:142
  9.5 54.4 %collective-permute-start.1 = (bf16[1,1,1,8,25,128]{5,4,3,2,1,0:T(8,128)(2,1)S(1)}, bf16[1,1,1,8,25,128]{5,4,3,2,1,0:T(8,128)(2,1)S(1)}, u32[]{:S(2)}, u32[]{:S(2)}) collective-permute-start(bf16[1,1,1,8,25,128]{5,4,3,2,1,0:T(8,128)(2,1)S(1)} %bitcast.173), channel_id=1, source_target_pairs={{8,0},{16,8},{24,16},{0,24},{9,1},{17,9},{25,17},{1,25},{10,2},{18... | collective-permute-start | bytes 153608 | tf_op jit(solution)/shard_map/ppermute | solution.py:22
  14.6 49.3 %collective-permute-start = (bf16[1,1,1,8,25,128]{5,4,3,2,1,0:T(8,128)(2,1)S(1)}, bf16[1,1,1,8,25,128]{5,4,3,2,1,0:T(8,128)(2,1)S(1)}, u32[]{:S(2)}, u32[]{:S(2)}) collective-permute-start(bf16[1,1,1,8,25,128]{5,4,3,2,1,0:T(8,128)(2,1)S(1)} %bitcast.174), channel_id=1, source_target_pairs={{0,8},{8,16},{16,24},{24,0},{1,9},{9,17},{17,25},{25,1},{2,10},{10... | collective-permute-start | bytes 153608 | tf_op jit(solution)/shard_map/ppermute | solution.py:19
  17.5 5.8 %copy-start.15 = (f32[1,1,1,3,512]{4,2,3,1,0:T(1,128)S(1)}, f32[1,1,1,3,512]{4,2,3,1,0:T(1,128)}, u32[]{:S(2)}) copy-start(f32[1,1,1,3,512]{4,2,3,1,0:T(1,128)} %param.21) | copy-start | bytes 18436
  17.5 5.9 %copy-start.20 = (s32[1,1,1,16,32]{4,3,2,1,0:T(8,128)S(1)}, s32[1,1,1,16,32]{4,3,2,1,0:T(8,128)}, u32[]{:S(2)}) copy-start(s32[1,1,1,16,32]{4,3,2,1,0:T(8,128)} %param.20) | copy-start | bytes 6148
  18.9 45.6 %copy-start.26 = (s32[5]{0:T(128)S(1)}, s32[5]{0:T(128)}, u32[]{:S(2)}) copy-start(s32[5]{0:T(128)} %constant.102) | copy-start | bytes 64
  18.9 45.6 %copy-start.24 = (s32[4]{0:T(128)S(1)}, s32[4]{0:T(128)}, u32[]{:S(2)}) copy-start(s32[4]{0:T(128)} %constant.104) | copy-start | bytes 52
  18.9 45.7 %copy-start.25 = (s32[4]{0:T(128)S(1)}, s32[4]{0:T(128)}, u32[]{:S(2)}) copy-start(s32[4]{0:T(128)} %constant.103) | copy-start | bytes 52
  23.2 50.8 %copy-start.22 = (s32[3]{0:T(128)S(1)}, s32[3]{0:T(128)}, u32[]{:S(2)}) copy-start(s32[3]{0:T(128)} %constant.106) | copy-start | bytes 40
  23.3 50.8 %copy-start.23 = (s32[3]{0:T(128)S(1)}, s32[3]{0:T(128)}, u32[]{:S(2)}) copy-start(s32[3]{0:T(128)} %constant.105) | copy-start | bytes 40
  23.3 51.1 %copy-start.8 = (bf16[640,640]{1,0:T(8,128)(2,1)S(1)}, bf16[640,640]{1,0:T(8,128)(2,1)}, u32[]{:S(2)}) copy-start(bf16[640,640]{1,0:T(8,128)(2,1)} %param.22) | copy-start | bytes 2457604
  63.9 3.6 %collective-permute-start.3 = (bf16[3,1,1,8,25,128]{5,4,3,2,1,0:T(8,128)(2,1)S(1)}, bf16[3,1,1,8,25,128]{5,4,3,2,1,0:T(8,128)(2,1)S(1)}, u32[]{:S(2)}, u32[]{:S(2)}) collective-permute-start(bf16[3,1,1,8,25,128]{5,4,3,2,1,0:T(8,128)(2,1)S(1)} %pad_maximum_fusion.3), channel_id=1, source_target_pairs={{2,0},{4,2},{6,4},{0,6},{3,1},{5,3},{7,5},{1,7},{10,8},{12,10},{14... | collective-permute-start | bytes 460808 | tf_op jit(solution)/shard_map/ppermute | solution.py:22
  64.0 7.7 %collective-permute-start.2 = (bf16[3,1,1,8,25,128]{5,4,3,2,1,0:T(8,128)(2,1)S(1)}, bf16[3,1,1,8,25,128]{5,4,3,2,1,0:T(8,128)(2,1)S(1)}, u32[]{:S(2)}, u32[]{:S(2)}) collective-permute-start(bf16[3,1,1,8,25,128]{5,4,3,2,1,0:T(8,128)(2,1)S(1)} %pad_maximum_fusion.3), channel_id=1, source_target_pairs={{0,2},{2,4},{4,6},{6,0},{1,3},{3,5},{5,7},{7,1},{8,10},{10,12},{12... | collective-permute-start | bytes 460808 | tf_op jit(solution)/shard_map/ppermute | solution.py:19
  72.0 14.0 %collective-permute-start.5 = (bf16[3,3,1,8,25,128]{5,3,4,2,1,0:T(8,128)(2,1)S(1)}, bf16[3,3,1,8,25,128]{5,3,4,2,1,0:T(8,128)(2,1)}, u32[]{:S(2)}, u32[]{:S(2)}) collective-permute-start(bf16[3,3,1,8,25,128]{5,3,4,2,1,0:T(8,128)(2,1)S(1)} %copy.50), channel_id=1, source_target_pairs={{1,0},{0,1},{3,2},{2,3},{5,4},{4,5},{7,6},{6,7},{9,8},{8,9},{11,10... | collective-permute-start | bytes 1382408 | tf_op jit(solution)/shard_map/ppermute | solution.py:22
  73.0 22.2 %collective-permute-start.4 = (bf16[3,3,1,8,25,128]{5,3,4,2,1,0:T(8,128)(2,1)S(1)}, bf16[3,3,1,8,25,128]{5,3,4,2,1,0:T(8,128)(2,1)}, u32[]{:S(2)}, u32[]{:S(2)}) collective-permute-start(bf16[3,3,1,8,25,128]{5,3,4,2,1,0:T(8,128)(2,1)S(1)} %copy.50), channel_id=1, source_target_pairs={{0,1},{1,0},{2,3},{3,2},{4,5},{5,4},{6,7},{7,6},{8,9},{9,8},{10,11... | collective-permute-start | bytes 1382408 | tf_op jit(solution)/shard_map/ppermute | solution.py:19
  135.7 3.2 %copy-start.4 = (f32[512,4,128]{0,2,1:T(8,128)S(1)}, f32[512,4,128]{0,2,1:T(8,128)}, u32[]{:S(2)}) copy-start(f32[512,4,128]{0,2,1:T(8,128)} %copy.61) | copy-start | bytes 3145732
  135.7 3.2 %copy-start.5 = (f32[512,4,128]{0,2,1:T(8,128)S(1)}, f32[512,4,128]{0,2,1:T(8,128)}, u32[]{:S(2)}) copy-start(f32[512,4,128]{0,2,1:T(8,128)} %copy.63) | copy-start | bytes 3145732
  142.4 4.2 %copy-start.13 = (f32[16,32]{1,0:T(8,128)S(1)}, f32[16,32]{1,0:T(8,128)}, u32[]{:S(2)}) copy-start(f32[16,32]{1,0:T(8,128)} %get-tuple-element.61) | copy-start | bytes 6148
  142.4 4.2 %copy-start.14 = (f32[16,32]{1,0:T(8,128)S(1)}, f32[16,32]{1,0:T(8,128)}, u32[]{:S(2)}) copy-start(f32[16,32]{1,0:T(8,128)} %get-tuple-element.62) | copy-start | bytes 6148
  144.0 6.6 %copy-start.10 = (bf16[1,1,1,16,25,128]{5,3,4,2,1,0:T(8,128)(2,1)S(1)}, bf16[1,1,1,16,25,128]{5,3,4,2,1,0:T(8,128)(2,1)}, u32[]{:S(2)}) copy-start(bf16[1,1,1,16,25,128]{5,3,4,2,1,0:T(8,128)(2,1)} %param.17) | copy-start | bytes 307204
  146.6 13.6 %copy-start.1 = (f32[1024,128]{1,0:T(8,128)S(1)}, f32[1024,128]{1,0:T(8,128)}, u32[]{:S(2)}) copy-start(f32[1024,128]{1,0:T(8,128)} %param.26) | copy-start | bytes 1572868
  160.2 3.3 %copy-start.3 = (f32[1024,128]{1,0:T(8,128)S(1)}, f32[1024,128]{1,0:T(8,128)}, u32[]{:S(2)}) copy-start(f32[1024,128]{1,0:T(8,128)} %get-tuple-element.31) | copy-start | bytes 1572868
  (10 other events, 23.5 us)
Sparse Core Ops, SparseCore 0:
  23.4 136.8 all-reduce.3
where the time goes:
time: 177 us; the launch traced here: 176 us
  local copies, waits for them, and re-layouts  41.7 us (24%)
  blocking collectives  40.4 us (23%)
  waiting for transfers between devices  33.1 us (19%)
  matrix products  21.6 us (12%)
  other arithmetic  17.1 us (10%)
  between operations  14.7 us (8%)
  starting transfers between devices  7.82 us (4%)
    psum x1, blocking collectives, local(): lax.psum((table_product(cos_table, charges), table_product(sin_table, cha...  40.4 us
    ppermute x3, waiting for transfers between devices, with_halo(): lax.ppermute(lax.slice_in_dim(block, block.shape[dim] - width, None, axis...  12.3 us
    ppermute x3, waiting for transfers between devices, with_halo(): lax.ppermute(lax.slice_in_dim(block, 0, width, axis=dim), axis, backward)  11.8 us
    psum x1, waiting for transfers between devices, local(): lax.psum((table_product(cos_table, charges), table_product(sin_table, cha...  8.93 us
    gather x2, local copies, waits for them, and re-layouts, edge_messages(): source = lookup_table[flat_index]  8.67 us
    dot_general x4, matrix products, table_product(): return jnp.dot(table.T, values, precision=highest)  7.14 us
    reduce_sum x2, other arithmetic, neighbour_sum(): jnp.sum(weighted.reshape(atom_count, neighbour_count, values.shape[1], fe...  6.74 us
    gather x2, local copies, waits for them, and re-layouts, edge_messages(): minus_part = source[:, minus_slots, :].astype(jnp.float32)  6.71 us
  transfers between devices with their start and end apart: 7, of which 5 were waited for; matrix products, arithmetic and copies ran while one was open for 39% of the time, Pallas kernels for 0%

commit v1 on v0

--- a/solution.py
+++ b/solution.py
@@ -140,14 +140,17 @@
     charges = local_irreps[:, 0, :].astype(jnp.float32)
     grad_input = cotangent[0, 0, 0]
     raw_cos, raw_sin, charge_total, plane_cos, plane_sin = lax.psum(
-        (
-            table_product(cos_table, charges),
-            table_product(sin_table, charges),
-            jnp.sum(charges, axis=0),
-            jnp.sum(cos_table, axis=0),
-            jnp.sum(sin_table, axis=0),
+        lax.psum(
+            (
+                table_product(cos_table, charges),
+                table_product(sin_table, charges),
+                jnp.sum(charges, axis=0),
+                jnp.sum(cos_table, axis=0),
+                jnp.sum(sin_table, axis=0),
+            ),
+            "gx",
         ),
-        ("gx", "gy", "gz"),
+        ("gy", "gz"),
     )
     resp_cos, resp_sin = lax.psum(
         (table_product(cos_table, grad_input), table_product(sin_table, grad_input)),

time: 177 us -> 288 us (1.63)
  waiting for transfers between devices: 33.1 us -> 148 us
  blocking collectives: 40.4 us -> 26.8 us
  other arithmetic: 17.1 us -> 21.7 us
    psum x0 -> x2, waiting for transfers between devices: none -> 144 us  [the longest x1 88.7 us: local(): lax.psum((table_product(cos_table, grad_input), table_product(sin_table,...]
    psum x1, blocking collectives: 40.4 us -> 12.6 us  [local(): lax.psum((table_product(cos_table, charges), table_product(sin_table, cha...]
    psum x0 -> x1, blocking collectives: none -> 14.2 us  [local(): lax.psum(lax.psum((table_product(cos_table, charges), table_product(sin_t...]
    ppermute x3, waiting for transfers between devices: 12.3 us -> 0.98 us  [with_halo(): lax.ppermute(lax.slice_in_dim(block, block.shape[dim] - width, None, axis...]
    psum x1, waiting for transfers between devices: 8.93 us -> 0.02 us  [local(): lax.psum((table_product(cos_table, charges), table_product(sin_table, cha...]
    ppermute x3, waiting for transfers between devices: 11.8 us -> 3.32 us  [with_halo(): lax.ppermute(lax.slice_in_dim(block, 0, width, axis=dim), axis, backward)]
  transfers between devices with their start and end apart: 7 -> 9, of which waited for: 5 -> 4; matrix products, arithmetic and copies ran while one was open for 39% -> 28% of each run, Pallas kernels for 0% -> 0%
where the time goes in v1:
time: 288 us; the launch traced here: 287 us
  waiting for transfers between devices  148 us (51%)
  local copies, waits for them, and re-layouts  42.8 us (15%)
  blocking collectives  26.8 us (9%)
  matrix products  24.4 us (8%)
  other arithmetic  21.7 us (8%)
  between operations  14.5 us (5%)
  starting transfers between devices  8.58 us (3%)
    psum x1, waiting for transfers between devices, local(): lax.psum((table_product(cos_table, grad_input), table_product(sin_table,...  88.7 us
    psum x1, waiting for transfers between devices, local(): lax.psum(lax.psum((table_product(cos_table, charges), table_product(sin_t...  55.2 us
    psum x1, blocking collectives, local(): lax.psum(lax.psum((table_product(cos_table, charges), table_product(sin_t...  14.2 us
    psum x1, blocking collectives, local(): lax.psum((table_product(cos_table, charges), table_product(sin_table, cha...  12.6 us
    gather x2, local copies, waits for them, and re-layouts, edge_messages(): source = lookup_table[flat_index]  8.78 us
    dot_general x4, matrix products, table_product(): return jnp.dot(table.T, values, precision=highest)  7.84 us
    reduce_sum x2, other arithmetic, neighbour_sum(): jnp.sum(weighted.reshape(atom_count, neighbour_count, values.shape[1], fe...  7.18 us
    ppermute x3, starting transfers between devices, with_halo(): lax.ppermute(lax.slice_in_dim(block, 0, width, axis=dim), axis, backward)  7.02 us
  transfers between devices with their start and end apart: 9, of which 4 were waited for; matrix products, arithmetic and copies ran while one was open for 28% of the time, Pallas kernels for 0%

profile of v1, /device:TPU:0, one launch (start us, length us, event | category | flops | bytes accessed | tf_op | source)
XLA Modules:
  0.0 287.2 jit_solution(5980326981510226291)
XLA Ops:
  9.5 5.1 %collective-permute-start.1 = (bf16[1,1,1,8,25,128]{5,4,3,2,1,0:T(8,128)(2,1)S(1)}, bf16[1,1,1,8,25,128]{5,4,3,2,1,0:T(8,128)(2,1)S(1)}, u32[]{:S(2)}, u32[]{:S(2)}) collective-permute-start(bf16[1,1,1,8,25,128]{5,4,3,2,1,0:T(8,128)(2,1)S(1)} %bitcast.173), channel_id=1, source_target_pairs={{8,0},{16,8},{24,16},{0,24},{9,1},{17,9},{25,17},{1,25},{10,2},{18... | collective-permute-start | bytes 153608 | tf_op jit(solution)/shard_map/ppermute | solution.py:22
  16.0 2.5 fusion.34
  18.5 2.5 fusion.36
  24.4 12.6 %all-reduce.3 = (f32[128]{0:T(128)S(1)}, f32[1024]{0:T(1024)S(1)}, f32[1024]{0:T(1024)S(1)}) all-reduce(f32[128]{0:T(128)S(1)} %get-tuple-element.38, f32[1024]{0:T(1024)S(1)} %reduce_sum.87, f32[1024]{0:T(1024)S(1)} %reduce_sum.89), channel_id=1, replica_groups=mesh['gx'=4,'gy'=4,'gz'=2] {'gx'}, use_global_device_ids=true, to_apply=%region_12.0 | all-reduce | flops 2176 | bytes 17408 | tf_op jit(solution)/shard_map/psum | solution.py:143
  37.0 14.2 %all-reduce.1 = (f32[128]{0:T(128)S(1)}, f32[1024]{0:T(1024)S(1)}, f32[1024]{0:T(1024)S(1)}) all-reduce(f32[128]{0:T(128)S(1)} %get-tuple-element.33, f32[1024]{0:T(1024)S(1)} %get-tuple-element.34, f32[1024]{0:T(1024)S(1)} %get-tuple-element.35), channel_id=1, replica_groups=mesh['gx'=4,'gy'=4,'gz'=2] {'gy','gz'}, use_global_device_ids=true, to_apply=%region_13.0 | all-reduce | flops 2176 | bytes 17408 | tf_op jit(solution)/shard_map/psum | solution.py:142
  57.6 3.3 %collective-permute-done.3 = bf16[3,1,1,8,25,128]{5,4,3,2,1,0:T(8,128)(2,1)S(1)} collective-permute-done((bf16[3,1,1,8,25,128]{5,4,3,2,1,0:T(8,128)(2,1)S(1)}, bf16[3,1,1,8,25,128]{5,4,3,2,1,0:T(8,128)(2,1)S(1)}, u32[]{:S(2)}, u32[]{:S(2)}) %collective-permute-start.3) | collective-permute-done | bytes 153632 | tf_op jit(solution)/shard_map/ppermute | solution.py:22
  65.2 88.7 %all-reduce.9.cloned.1.call-done = (f32[1024,128]{1,0:T(8,128)}, f32[1024,128]{1,0:T(8,128)}) async-done(((f32[1024,128]{1,0:T(8,128)}, f32[1024,128]{1,0:T(8,128)}), (f32[1024,128]{1,0:T(8,128)}, f32[1024,128]{1,0:T(8,128)})) %all-reduce.9.cloned.1.call-update) | async-done | bytes 1048592 | tf_op jit(solution)/shard_map/psum | solution.py:155
  153.9 1.5 convolution_bitcast_fusion.3
  161.0 3.6 %gather_fusion.1 = bf16[512,25,128]{2,1,0:T(8,128)(2,1)} fusion(bf16[232,25,128]{2,1,0:T(8,128)(2,1)S(1)} %pad_maximum_fusion, s32[1024]{0:T(1024)} %get-tuple-element.80), kind=kCustom, calls=%fused_computation.1 | custom fusion | bytes 6555648 | tf_op jit(solution)/shard_map/gather | solution.py:47
  164.6 5.2 %copy.56 = bf16[512,25,128]{2,0,1:T(8,128)(2,1)} copy(bf16[512,25,128]{2,1,0:T(8,128)(2,1)} %gather_fusion.1) | data formatting | bytes 6553600 | tf_op jit(solution)/shard_map/gather | solution.py:47
  169.8 3.4 %gather_fusion.6 = bf16[3,512,128]{2,1,0:T(8,128)(2,1)} fusion(bf16[512,25,128]{2,0,1:T(8,128)(2,1)} %copy.56, s32[1024]{0:T(1024)} %get-tuple-element.75), kind=kCustom, calls=%fused_computation.6 | custom fusion | bytes 786444 | tf_op jit(solution)/shard_map/gather | solution.py:79
  173.2 2.7 gather_fusion.5
  178.5 3.5 %gather_fusion.4 = bf16[4,512,128]{2,1,0:T(8,128)(2,1)} fusion(bf16[512,25,128]{2,0,1:T(8,128)(2,1)} %copy.56, s32[1024]{0:T(1024)} %get-tuple-element.77), kind=kCustom, calls=%fused_computation.4 | custom fusion | bytes 1048592 | tf_op jit(solution)/shard_map/gather | solution.py:79
  181.9 3.4 %gather_fusion.3 = bf16[4,512,128]{2,1,0:T(8,128)(2,1)} fusion(bf16[512,25,128]{2,0,1:T(8,128)(2,1)} %copy.56, s32[1024]{0:T(1024)} %get-tuple-element.78), kind=kCustom, calls=%fused_computation.3 | custom fusion | bytes 1048592 | tf_op jit(solution)/shard_map/gather | solution.py:78
  185.4 2.8 gather_fusion.2
  189.3 2.2 bitcast_reduce_fusion
  202.2 3.8 %multiply_reduce_fusion = (f32[16,3,128]{2,1,0:T(4,128)S(1)}, f32[16,3,128]{2,1,0:T(4,128)S(1)}) fusion(f32[16,32,3,128]{3,2,1,0:T(4,128)} %reshape.294, f32[16,32,3,128]{3,2,1,0:T(4,128)S(1)} %reshape.293, f32[16,32]{1,0:T(8,128)S(1)} %div.88, f32[16,32]{1,0:T(8,128)S(1)} %copy-done.25, f32[16,32]{1,0:T(8,128)S(1)} %copy-done.24), kind=kLoop, calls=%fused_computation.50 | loop fusion | flops 1953792 | bytes 1628160 | tf_op jit(solution)/shard_map/reduce_sum | solution.py:58
  207.7 1.8 slice_subtract_fusion
  209.5 1.6 reshape.291
  211.2 2.6 reshape.292
  213.8 3.4 %multiply_reduce_fusion.2 = (f32[16,4,128]{2,1,0:T(4,128)S(1)}, f32[16,4,128]{2,1,0:T(4,128)S(1)}) fusion(f32[16,32,4,128]{3,2,1,0:T(4,128)} %reshape.292, f32[16,32,4,128]{3,2,1,0:T(4,128)S(1)} %reshape.291, f32[16,32]{1,0:T(8,128)S(1)} %div.88, f32[16,32]{1,0:T(8,128)S(1)} %copy-done.22, f32[16,32]{1,0:T(8,128)S(1)} %copy-done.23), kind=kLoop, calls=%fused_computation.52 | loop fusion | flops 2605056 | bytes 2168832 | tf_op jit(solution)/shard_map/reduce_sum | solution.py:58
  218.3 55.2 %all-reduce.11.cloned.1.call-done = (f32[1024,128]{1,0:T(8,128)}, f32[1024,128]{1,0:T(8,128)}) async-done(((f32[1024,128]{1,0:T(8,128)}, f32[1024,128]{1,0:T(8,128)}), (f32[1024,128]{1,0:T(8,128)}, f32[1024,128]{1,0:T(8,128)})) %all-reduce.11.cloned.1.call-update) | async-done | bytes 1048592 | tf_op jit(solution)/shard_map/psum | solution.py:142
  273.5 1.6 fusion.29
  275.1 1.8 convolution_bitcast_fusion
  (186 shorter events, 43.6 us)
Async XLA Ops:
  7.2 199.2 %copy-start = (bf16[512,1024]{1,0:T(8,128)(2,1)S(1)}, bf16[512,1024]{1,0:T(8,128)(2,1)}, u32[]{:S(2)}) copy-start(bf16[512,1024]{1,0:T(8,128)(2,1)} %param.23) | copy-start | bytes 3145732
  7.2 146.7 %all-reduce.9.cloned.1.call-start = ((), (), s32[]{:S(2)}) async-start(), calls=%async_computation | async-start | bytes 2097152 | tf_op jit(solution)/shard_map/psum | solution.py:155
  9.5 44.1 %collective-permute-start.1 = (bf16[1,1,1,8,25,128]{5,4,3,2,1,0:T(8,128)(2,1)S(1)}, bf16[1,1,1,8,25,128]{5,4,3,2,1,0:T(8,128)(2,1)S(1)}, u32[]{:S(2)}, u32[]{:S(2)}) collective-permute-start(bf16[1,1,1,8,25,128]{5,4,3,2,1,0:T(8,128)(2,1)S(1)} %bitcast.173), channel_id=1, source_target_pairs={{8,0},{16,8},{24,16},{0,24},{9,1},{17,9},{25,17},{1,25},{10,2},{18... | collective-permute-start | bytes 153608 | tf_op jit(solution)/shard_map/ppermute | solution.py:22
  14.6 39.0 %collective-permute-start = (bf16[1,1,1,8,25,128]{5,4,3,2,1,0:T(8,128)(2,1)S(1)}, bf16[1,1,1,8,25,128]{5,4,3,2,1,0:T(8,128)(2,1)S(1)}, u32[]{:S(2)}, u32[]{:S(2)}) collective-permute-start(bf16[1,1,1,8,25,128]{5,4,3,2,1,0:T(8,128)(2,1)S(1)} %bitcast.174), channel_id=1, source_target_pairs={{0,8},{8,16},{16,24},{24,0},{1,9},{9,17},{17,25},{25,1},{2,10},{10... | collective-permute-start | bytes 153608 | tf_op jit(solution)/shard_map/ppermute | solution.py:19
  16.0 141.3 %copy-start.8 = (f32[16,1024]{1,0:T(8,128)}, f32[16,1024]{1,0:T(8,128)S(1)}, u32[]{:S(2)}) copy-start(f32[16,1024]{1,0:T(8,128)S(1)} %get-tuple-element.48) | copy-start | bytes 196612
  21.1 31.9 %copy-start.40 = (s32[5]{0:T(128)S(1)}, s32[5]{0:T(128)}, u32[]{:S(2)}) copy-start(s32[5]{0:T(128)} %constant.102) | copy-start | bytes 64
  21.1 33.8 %copy-start.38 = (s32[4]{0:T(128)S(1)}, s32[4]{0:T(128)}, u32[]{:S(2)}) copy-start(s32[4]{0:T(128)} %constant.104) | copy-start | bytes 52
  21.1 33.8 %copy-start.39 = (s32[4]{0:T(128)S(1)}, s32[4]{0:T(128)}, u32[]{:S(2)}) copy-start(s32[4]{0:T(128)} %constant.103) | copy-start | bytes 52
  21.1 34.5 %copy-start.14 = (bf16[640,640]{1,0:T(8,128)(2,1)S(1)}, bf16[640,640]{1,0:T(8,128)(2,1)}, u32[]{:S(2)}) copy-start(bf16[640,640]{1,0:T(8,128)(2,1)} %param.22) | copy-start | bytes 2457604
  21.1 196.4 %all-reduce.13.cloned.1.call-start = ((), (), s32[]{:S(2)}) async-start(), calls=%async_computation.2 | async-start | bytes 2097152 | tf_op jit(solution)/shard_map/psum | solution.py:143
  22.6 34.4 %copy-start.36 = (s32[3]{0:T(128)S(1)}, s32[3]{0:T(128)}, u32[]{:S(2)}) copy-start(s32[3]{0:T(128)} %constant.106) | copy-start | bytes 40
  22.6 34.4 %copy-start.37 = (s32[3]{0:T(128)S(1)}, s32[3]{0:T(128)}, u32[]{:S(2)}) copy-start(s32[3]{0:T(128)} %constant.105) | copy-start | bytes 40
  24.0 249.5 %all-reduce.11.cloned.1.call-start = ((), (), s32[]{:S(2)}) async-start(), calls=%async_computation.1 | async-start | bytes 2097152 | tf_op jit(solution)/shard_map/psum | solution.py:142
  24.3 38.8 %copy-start.33 = (f32[512]{0:T(512)}, f32[512]{0:T(512)S(1)}, u32[]{:S(2)}) copy-start(f32[512]{0:T(512)S(1)} %exponential_multiply_fusion) | copy-start | bytes 6148
  51.2 102.7 %copy-start.20 = (f32[1024]{0:T(1024)}, f32[1024]{0:T(1024)S(1)}, u32[]{:S(2)}) copy-start(f32[1024]{0:T(1024)S(1)} %get-tuple-element.29) | copy-start | bytes 12292
  53.7 7.2 %collective-permute-start.3 = (bf16[3,1,1,8,25,128]{5,4,3,2,1,0:T(8,128)(2,1)S(1)}, bf16[3,1,1,8,25,128]{5,4,3,2,1,0:T(8,128)(2,1)S(1)}, u32[]{:S(2)}, u32[]{:S(2)}) collective-permute-start(bf16[3,1,1,8,25,128]{5,4,3,2,1,0:T(8,128)(2,1)S(1)} %pad_maximum_fusion.3), channel_id=1, source_target_pairs={{2,0},{4,2},{6,4},{0,6},{3,1},{5,3},{7,5},{1,7},{10,8},{12,10},{14... | collective-permute-start | bytes 460808 | tf_op jit(solution)/shard_map/ppermute | solution.py:22
  54.9 7.0 %collective-permute-start.2 = (bf16[3,1,1,8,25,128]{5,4,3,2,1,0:T(8,128)(2,1)S(1)}, bf16[3,1,1,8,25,128]{5,4,3,2,1,0:T(8,128)(2,1)}, u32[]{:S(2)}, u32[]{:S(2)}) collective-permute-start(bf16[3,1,1,8,25,128]{5,4,3,2,1,0:T(8,128)(2,1)S(1)} %pad_maximum_fusion.3), channel_id=1, source_target_pairs={{0,2},{2,4},{4,6},{6,0},{1,3},{3,5},{5,7},{7,1},{8,10},{10,12},{12... | collective-permute-start | bytes 460808 | tf_op jit(solution)/shard_map/ppermute | solution.py:19
  55.6 98.3 %copy-start.1 = (f32[1024,128]{1,0:T(8,128)S(1)}, f32[1024,128]{1,0:T(8,128)}, u32[]{:S(2)}) copy-start(f32[1024,128]{1,0:T(8,128)} %param.26) | copy-start | bytes 1572868
  63.1 95.2 %collective-permute-start.5 = (bf16[3,3,1,8,25,128]{5,3,4,2,1,0:T(8,128)(2,1)S(1)}, bf16[3,3,1,8,25,128]{5,3,4,2,1,0:T(8,128)(2,1)}, u32[]{:S(2)}, u32[]{:S(2)}) collective-permute-start(bf16[3,3,1,8,25,128]{5,3,4,2,1,0:T(8,128)(2,1)S(1)} %copy.50), channel_id=1, source_target_pairs={{1,0},{0,1},{3,2},{2,3},{5,4},{4,5},{7,6},{6,7},{9,8},{8,9},{11,10... | collective-permute-start | bytes 1382408 | tf_op jit(solution)/shard_map/ppermute | solution.py:22
  63.7 95.7 %collective-permute-start.4 = (bf16[3,3,1,8,25,128]{5,3,4,2,1,0:T(8,128)(2,1)S(1)}, bf16[3,3,1,8,25,128]{5,3,4,2,1,0:T(8,128)(2,1)S(1)}, u32[]{:S(2)}, u32[]{:S(2)}) collective-permute-start(bf16[3,3,1,8,25,128]{5,3,4,2,1,0:T(8,128)(2,1)S(1)} %copy.50), channel_id=1, source_target_pairs={{0,1},{1,0},{2,3},{3,2},{4,5},{5,4},{6,7},{7,6},{8,9},{9,8},{10,11... | collective-permute-start | bytes 1382408 | tf_op jit(solution)/shard_map/ppermute | solution.py:19
  213.7 59.8 %copy-start.21 = (f32[1024]{0:T(1024)S(1)}, f32[1024]{0:T(1024)}, u32[]{:S(2)}) copy-start(f32[1024]{0:T(1024)} %copy-done.20) | copy-start | bytes 12292
  213.8 59.7 %copy-start.26 = (f32[128]{0:T(128)S(1)}, f32[128]{0:T(128)}, u32[]{:S(2)}) copy-start(f32[128]{0:T(128)} %broadcast_multiply_fusion) | copy-start | bytes 1540
  217.2 57.9 %copy-start.18 = (f32[1,1,1,16,128]{4,3,2,1,0:T(8,128)S(1)}, f32[1,1,1,16,128]{4,3,2,1,0:T(8,128)}, u32[]{:S(2)}) copy-start(f32[1,1,1,16,128]{4,3,2,1,0:T(8,128)} %param.27) | copy-start | bytes 24580
  217.6 60.0 %copy-start.9 = (f32[16,1024]{1,0:T(8,128)S(1)}, f32[16,1024]{1,0:T(8,128)}, u32[]{:S(2)}) copy-start(f32[16,1024]{1,0:T(8,128)} %copy-done.8) | copy-start | bytes 196612
  (26 other events, 102.8 us)
Sparse Core Ops, SparseCore 0:
  21.2 132.6 all-reduce.8
  156.3 50.9 all-reduce.12
  217.7 55.7 all-reduce.10
